TPU v7x, 256 devices: a whole 4x4x8 slice. The times are simulated.
256 devices in a mesh: bx: 4 (over x), by: 32 (over y, z), gz: 2 (over core).
Axes of the slice: x: 4, y: 4, z: 8, core: 2. Of those that a mesh axis runs over, the one named last changes fastest.
Arguments:
- electric_start: float32 [3, 512, 64, 256], P(None, 'by', 'bx', 'gz'), may hold values from -6 to 6
- magnetic_start: float32 [3, 512, 64, 256], P(None, 'by', 'bx', 'gz'), may hold values from -6 to 6
- current_start: float32 [3, 512, 64, 256], P(None, 'by', 'bx', 'gz'), may hold values from -6 to 6
- cotangent: float32 [3, 512, 64, 256], P(None, 'by', 'bx', 'gz'), may hold values from -6 to 6
- level_set: float32 [512, 64, 256], P('by', 'bx', 'gz'), may hold values from -8 to 8
- material: int32 [512, 64, 256], P('by', 'bx', 'gz'), may hold values from 0 to 2
- source_cell: int32 [2048], P(('bx', 'by', 'gz')), may hold values from 0 to 32767
- basis: bfloat16 [65536, 64, 256], P(('bx', 'by', 'gz')), may hold values from 0 to 1
- block_owner: int32 [65536, 1], P(('bx', 'by', 'gz')), may hold values from 0 to 127; in each aligned block of 256 rows (0 to 255, 256 to 511, ...) at most 4 rows name the same one
- block_group: int32 [65536], P(('bx', 'by', 'gz')), may hold values from 0 to 127
Outputs:
- final_electric: float32 [3, 512, 64, 256], P(None, 'by', 'bx', 'gz')
- adjoint_electric: float32 [3, 512, 64, 256], P(None, 'by', 'bx', 'gz')
- coef_grad: float32 [64, 32768], P(None, ('bx', 'by', 'gz'))
Inputs may be any that keep to these rules, and one draw needn't show every extreme that they name: `material`: 0 is vacuum, 1 design dielectric, 2 silver. `source_cell`: a flat cell index within the device's own brick; a cell may be named more than once. `block_owner`: among the 256 blocks of one device no owner is named by more than 4 blocks, and in some device one owner is named by exactly 4.
All inputs are finite; a program needn't handle non-finite values.
Results may differ from a plain program's by a relative error of at most 0.0029.
Values sent between devices are 32-bit elements; how exact they have to be, the bound alone decides.
A program may use at most 64 MiB of HBM per device.

v0:
```python
import jax
import jax.numpy as jnp
from jax import lax
from jax.sharding import PartitionSpec as P

NSTEP = 2
KB = 64
GRP_DEV = 128
time_step = 0.5
drude_keep = 0.9
drude_gain = 1.0
metal_permit = 3.0
design_contrast = 5.0
source_level = 3.0
source_wave = (1.0, -0.6, 0.8, -0.4)


def passed_along(x, axis, by):
    count = lax.axis_size(axis)
    pairs = [(i, i + by) for i in range(count) if 0 <= i + by < count]
    return lax.ppermute(x, axis, pairs)


def face_y(face_cells, offset):
    return passed_along(face_cells, "by", offset)


def face_x(face_cells, offset):
    return passed_along(face_cells, "bx", offset)


def face_z(face_cells, offset):
    return passed_along(face_cells, "gz", offset)


def beside(couple, axis_dim, offset):
    length = couple.shape[axis_dim]
    border_at = 0 if offset < 0 else length - 1
    face_cells = lax.index_in_dim(couple, border_at, axis=axis_dim, keepdims=False)
    if axis_dim == 1:
        arrived = face_y(face_cells, offset)
    elif axis_dim == 2:
        arrived = face_x(face_cells, offset)
    else:
        flattened = face_cells.reshape(face_cells.shape[0], -1)
        arrived = face_z(flattened, offset).reshape(face_cells.shape)
    arrived = jnp.expand_dims(arrived, axis_dim)
    if offset < 0:
        return jnp.concatenate(
            [lax.slice_in_dim(couple, 1, length, axis=axis_dim), arrived], axis=axis_dim
        )
    return jnp.concatenate(
        [arrived, lax.slice_in_dim(couple, 0, length - 1, axis=axis_dim)], axis=axis_dim
    )


def differ(couple, axis_dim, offset):
    neighbour = beside(couple, axis_dim, offset)
    if offset < 0:
        return neighbour - couple
    return couple - neighbour


def curl(fields, offset):
    along_x = differ(jnp.stack([fields[1], fields[2]]), 2, offset)
    along_y = differ(jnp.stack([fields[0], fields[2]]), 1, offset)
    along_z = differ(jnp.stack([fields[0], fields[1]]), 3, offset)
    return jnp.stack([along_y[1] - along_z[1], along_z[0] - along_x[1], along_x[0] - along_y[0]])


def local(
    electric_start,
    magnetic_start,
    current_start,
    cotangent,
    level_set,
    material,
    source_cell,
    basis,
    block_owner,
    block_group,
):
    silver = (material == 2).astype(jnp.float32)
    design = (material == 1).astype(jnp.float32)
    smooth = jax.nn.sigmoid(level_set)
    permit = jnp.where(
        material == 2, metal_permit, jnp.where(material == 1, 1.0 + design_contrast * smooth, 1.0)
    )
    sources = (
        jnp.zeros((material.size,), jnp.float32).at[source_cell].add(1.0).reshape(material.shape)
    )
    electric, magnetic, current = (electric_start, magnetic_start, current_start)
    drives = []
    for moment in range(NSTEP):
        magnetic = magnetic - time_step * curl(electric, -1)
        current = silver * (drude_keep * current + drude_gain * electric)
        drive_term = curl(magnetic, 1) - current
        electric = electric + time_step / permit * drive_term
        electric = electric.at[2].add(source_level * source_wave[moment] * sources)
        drives.append(drive_term)
    step_ratio = time_step / permit
    adj_electric = cotangent
    adj_magnetic = jnp.zeros_like(cotangent)
    adj_current = jnp.zeros_like(cotangent)
    eps_grad = jnp.zeros(material.shape, jnp.float32)
    for moment in reversed(range(NSTEP)):
        scaled = step_ratio * adj_electric
        eps_grad = eps_grad - jnp.sum(scaled * drives[moment], axis=0) / permit
        adj_drive = adj_current - scaled
        adj_magnetic = adj_magnetic + curl(scaled, -1)
        adj_electric = (
            adj_electric + drude_gain * silver * adj_drive - time_step * curl(adj_magnetic, 1)
        )
        adj_current = drude_keep * silver * adj_drive
    level_grad = eps_grad * design * design_contrast * (smooth * (1.0 - smooth))
    cell_grad = level_grad.astype(jnp.bfloat16)
    tile_width = basis.shape[2]
    tile_count = cell_grad.size // tile_width
    block_count = basis.shape[0]
    tile_fan = block_count // tile_count
    cell_tiles = cell_grad.reshape(tile_count, tile_width)
    blocks = basis.reshape(tile_count, tile_fan, KB, tile_width)
    partials = jnp.einsum(
        "tfkc,tc->tfk", blocks, cell_tiles, preferred_element_type=jnp.float32
    ).reshape(block_count, KB)
    size_bx = lax.axis_size("bx")
    planes = size_bx * lax.axis_size("by")
    capacity = max(2, 2 * block_count // planes)
    slots = planes * capacity
    owner_plane = block_owner[:, 0]
    owner_hits = (owner_plane[:, None] == jnp.arange(planes, dtype=jnp.int32)[None, :]).astype(
        jnp.float32
    )
    before = jnp.cumsum(owner_hits, axis=0) - owner_hits
    slot_rank = jnp.sum(before * owner_hits, axis=1).astype(jnp.int32)
    target = owner_plane * capacity + slot_rank
    placing = (target[:, None] == jnp.arange(slots, dtype=jnp.int32)[None, :]).astype(jnp.float32)
    send_vals = jnp.einsum("bk,bs->ks", partials, placing, precision=lax.Precision.HIGHEST)
    send_ids = (
        jnp.einsum(
            "b,bs->s",
            block_group.astype(jnp.float32) + 1.0,
            placing,
            precision=lax.Precision.HIGHEST,
        )[None, :]
        - 1.0
    )
    got_vals, got_ids = (
        lax.all_to_all(send_vals, ("bx", "by"), split_axis=1, concat_axis=1, tiled=True),
        lax.all_to_all(send_ids, ("bx", "by"), split_axis=1, concat_axis=1, tiled=True),
    )
    group_hits = (
        got_ids[0][:, None] == jnp.arange(GRP_DEV, dtype=jnp.int32)[None, :].astype(jnp.float32)
    ).astype(jnp.float32)
    coef_grad = jnp.dot(got_vals, group_hits, precision=lax.Precision.HIGHEST)
    return (electric, adj_electric, coef_grad)


def solution(mesh):
    return jax.shard_map(
        local,
        mesh=mesh,
        in_specs=(
            P(None, "by", "bx", "gz"),
            P(None, "by", "bx", "gz"),
            P(None, "by", "bx", "gz"),
            P(None, "by", "bx", "gz"),
            P("by", "bx", "gz"),
            P("by", "bx", "gz"),
            P(("bx", "by", "gz")),
            P(("bx", "by", "gz"), None, None),
            P(("bx", "by", "gz"), None),
            P(("bx", "by", "gz")),
        ),
        out_specs=(
            P(None, "by", "bx", "gz"),
            P(None, "by", "bx", "gz"),
            P(None, ("bx", "by", "gz")),
        ),
        check_vma=False,
    )
```

profile of v0, /device:TPU:4, one launch (start us, length us, event | category | flops | bytes accessed | tf_op | source)
XLA Modules:
  0.0 176.0 jit_solution(5927105462938856978)
XLA Ops:
  0.6 1.0 fusion.69
  1.7 1.3 collective-permute-start
  3.0 1.1 slice_reduce_fusion.6
  4.2 1.4 collective-permute-start.1
  5.6 0.9 slice.468
  6.5 2.4 %collective-permute-start.2 = (f32[2,16,128]{2,1,0:T(8,128)S(1)}, f32[2,16,128]{2,1,0:T(8,128)S(1)}, u32[]{:S(2)}, u32[]{:S(2)}) collective-permute-start(f32[2,16,128]{2,1,0:T(8,128)S(1)} %bitcast.135), channel_id=1, source_target_pairs={{64,0},{128,64},{192,128},{65,1},{129,65},{193,129},{66,2},{130,66... | collective-permute-start | bytes 49160 | tf_op jit(solution)/shard_map/ppermute | solution.py:21
  13.4 16.9 %all-to-all-start.1 = ((f32[1,128,4]{2,0,1:T(1,128)}), f32[1,128,4]{2,0,1:T(1,128)S(1)}, u32[]{:S(2)}, u32[]{:S(2)}) async-start(f32[1,128,4]{2,0,1:T(1,128)} %bitcast.57), calls=%async_computation.1 | async-start | bytes 131072 | tf_op jit(solution)/shard_map/all_to_all | solution.py:150
  31.0 1.6 broadcast_select_fusion
  34.6 1.6 fusion.42
  36.7 1.1 slice.463
  37.8 1.0 slice.467
  39.1 1.5 all-to-all-done.1
  42.7 1.2 maximum_subtract_fusion.2
  45.2 1.0 fusion.3
  47.1 2.6 %collective-permute-start.3 = (f32[2,16,128]{2,1,0:T(8,128)}, f32[2,16,128]{2,1,0:T(8,128)S(1)}, u32[]{:S(2)}, u32[]{:S(2)}) collective-permute-start(f32[2,16,128]{2,1,0:T(8,128)} %fusion.58), channel_id=1, source_target_pairs={{0,2},{2,4},{4,6},{6,8},{8,10},{10,12},{12,14},{14,16},{16,18},{18... | collective-permute-start | bytes 49160 | tf_op jit(solution)/shard_map/ppermute | solution.py:21
  49.8 1.9 %collective-permute-start.4 = (f32[2,256]{1,0:T(2,128)S(1)}, f32[2,256]{1,0:T(2,128)}, u32[]{:S(2)}, u32[]{:S(2)}) collective-permute-start(f32[2,256]{1,0:T(2,128)S(1)} %reshape_squeeze.25), channel_id=1, source_target_pairs={{0,1},{2,3},{4,5},{6,7},{8,9},{10,11},{12,13},{14,15},{16,17},{18,... | collective-permute-start | bytes 6152 | tf_op jit(solution)/shard_map/ppermute | solution.py:21
  52.4 3.1 %collective-permute-start.5 = (f32[2,16,128]{2,1,0:T(8,128)}, f32[2,16,128]{2,1,0:T(8,128)S(1)}, u32[]{:S(2)}, u32[]{:S(2)}) collective-permute-start(f32[2,16,128]{2,1,0:T(8,128)} %bitcast.8), channel_id=1, source_target_pairs={{0,64},{64,128},{128,192},{1,65},{65,129},{129,193},{2,66},{66,130... | collective-permute-start | bytes 49160 | tf_op jit(solution)/shard_map/ppermute | solution.py:21
  56.5 1.7 collective-permute-done.5
  58.6 1.0 constant_dynamic-update-slice_fusion
  60.6 1.3 collective-permute-start.6
  62.0 1.3 collective-permute-start.7
  63.3 1.3 collective-permute-start.13
  69.7 3.0 %collective-permute-start.8 = (f32[2,16,128]{2,1,0:T(8,128)S(1)}, f32[2,16,128]{2,1,0:T(8,128)S(1)}, u32[]{:S(2)}, u32[]{:S(2)}) collective-permute-start(f32[2,16,128]{2,1,0:T(8,128)S(1)} %bitcast.136), channel_id=1, source_target_pairs={{64,0},{128,64},{192,128},{65,1},{129,65},{193,129},{66,2},{130,66... | collective-permute-start | bytes 49160 | tf_op jit(solution)/shard_map/ppermute | solution.py:21
  72.7 1.3 collective-permute-start.12
  74.0 1.9 %collective-permute-start.14 = (f32[2,16,128]{2,1,0:T(8,128)}, f32[2,16,128]{2,1,0:T(8,128)S(1)}, u32[]{:S(2)}, u32[]{:S(2)}) collective-permute-start(f32[2,16,128]{2,1,0:T(8,128)} %bitcast.25), channel_id=1, source_target_pairs={{64,0},{128,64},{192,128},{65,1},{129,65},{193,129},{66,2},{130,66... | collective-permute-start | bytes 49160 | tf_op jit(solution)/shard_map/ppermute | solution.py:21
  75.9 0.9 broadcast_in_dim_reshape.34
  76.8 0.9 broadcast_in_dim_reshape.36
  77.7 1.0 fusion.15
  78.7 1.3 slice_subtract_fusion.9
  80.0 1.1 fusion.4
  82.1 1.0 fusion.13
  83.2 1.3 slice_subtract_fusion.5
  86.2 5.2 %collective-permute-start.9 = (f32[2,16,128]{2,1,0:T(8,128)S(1)}, f32[2,16,128]{2,1,0:T(8,128)S(1)}, u32[]{:S(2)}, u32[]{:S(2)}) collective-permute-start(f32[2,16,128]{2,1,0:T(8,128)S(1)} %fusion.60), channel_id=1, source_target_pairs={{0,2},{2,4},{4,6},{6,8},{8,10},{10,12},{12,14},{14,16},{16,18},{18... | collective-permute-start | bytes 49160 | tf_op jit(solution)/shard_map/ppermute | solution.py:21
  91.5 2.5 %collective-permute-start.10 = (f32[2,256]{1,0:T(2,128)S(1)}, f32[2,256]{1,0:T(2,128)S(1)}, u32[]{:S(2)}, u32[]{:S(2)}) collective-permute-start(f32[2,256]{1,0:T(2,128)S(1)} %reshape_squeeze.27), channel_id=1, source_target_pairs={{0,1},{2,3},{4,5},{6,7},{8,9},{10,11},{12,13},{14,15},{16,17},{18,... | collective-permute-start | bytes 6152 | tf_op jit(solution)/shard_map/ppermute | solution.py:21
  94.0 1.3 collective-permute-start.16
  96.8 3.6 %collective-permute-start.11 = (f32[2,16,128]{2,1,0:T(8,128)S(1)}, f32[2,16,128]{2,1,0:T(8,128)S(1)}, u32[]{:S(2)}, u32[]{:S(2)}) collective-permute-start(f32[2,16,128]{2,1,0:T(8,128)S(1)} %bitcast.137), channel_id=1, source_target_pairs={{0,64},{64,128},{128,192},{1,65},{65,129},{129,193},{2,66},{66,130... | collective-permute-start | bytes 49160 | tf_op jit(solution)/shard_map/ppermute | solution.py:21
  100.4 1.9 %collective-permute-start.17 = (f32[2,16,128]{2,1,0:T(8,128)S(1)}, f32[2,16,128]{2,1,0:T(8,128)S(1)}, u32[]{:S(2)}, u32[]{:S(2)}) collective-permute-start(f32[2,16,128]{2,1,0:T(8,128)S(1)} %bitcast.129), channel_id=1, source_target_pairs={{0,64},{64,128},{128,192},{1,65},{65,129},{129,193},{2,66},{66,130... | collective-permute-start | bytes 49160 | tf_op jit(solution)/shard_map/ppermute | solution.py:21
  102.4 3.6 %collective-permute-start.15 = (f32[2,16,128]{2,1,0:T(8,128)S(1)}, f32[2,16,128]{2,1,0:T(8,128)S(1)}, u32[]{:S(2)}, u32[]{:S(2)}) collective-permute-start(f32[2,16,128]{2,1,0:T(8,128)S(1)} %fusion.56), channel_id=1, source_target_pairs={{0,2},{2,4},{4,6},{6,8},{8,10},{10,12},{12,14},{14,16},{16,18},{18... | collective-permute-start | bytes 49160 | tf_op jit(solution)/shard_map/ppermute | solution.py:21
  106.9 0.9 broadcast_in_dim_reshape.37
  107.8 1.0 fusion.14
  108.8 1.3 slice_subtract_fusion.7
  110.2 1.2 fusion.18
  111.5 1.3 multiply_reduce_fusion.1
  113.0 1.1 fusion.35
  114.7 1.3 collective-permute-start.18
  116.7 1.5 collective-permute-start.19
  118.1 6.7 %fusion.70 = f32[128,1,2,64]{3,1,2,0:T(1,128)S(1)} fusion(bf16[128,256,1,1]{1,2,3,0:T(2,128)(2,1)S(1)} %reshape.178, bf16[128,2,64,256]{3,2,1,0:T(8,128)(2,1)} %bitcast.110), kind=kOutput, calls=%fused_computation.204 | convolution fusion | flops 8388608 | bytes 8519680 | tf_op jit(solution)/shard_map/tfkc,tc->tfk/dot_general | solution.py:123
  124.9 1.2 fusion
  128.4 1.9 %reshape.198 = f32[128,1,256]{2,1,0:T(1,128)} reshape(f32[128,4,64]{2,1,0:T(4,128)} %bitcast.112) | data formatting | bytes 262144
  130.3 17.0 %all-to-all-start = ((f32[128,1,256]{2,1,0:T(1,128)}), f32[128,1,256]{2,1,0:T(1,128)}, u32[]{:S(2)}, u32[]{:S(2)}) async-start(f32[128,1,256]{2,1,0:T(1,128)} %reshape.198), calls=%async_computation | async-start | bytes 262144 | tf_op jit(solution)/shard_map/all_to_all | solution.py:149
  147.3 2.3 %collective-permute-start.20 = (f32[2,16,128]{2,1,0:T(8,128)}, f32[2,16,128]{2,1,0:T(8,128)S(1)}, u32[]{:S(2)}, u32[]{:S(2)}) collective-permute-start(f32[2,16,128]{2,1,0:T(8,128)} %bitcast.138), channel_id=1, source_target_pairs={{64,0},{128,64},{192,128},{65,1},{129,65},{193,129},{66,2},{130,66... | collective-permute-start | bytes 49160 | tf_op jit(solution)/shard_map/ppermute | solution.py:21
  149.5 1.6 broadcast_in_dim_reshape.38
  151.1 1.0 fusion.8
  152.1 1.3 collective-permute-done.20
  153.4 1.1 slice_subtract_fusion.3
  156.2 3.3 %collective-permute-start.21 = (f32[2,16,128]{2,1,0:T(8,128)}, f32[2,16,128]{2,1,0:T(8,128)S(1)}, u32[]{:S(2)}, u32[]{:S(2)}) collective-permute-start(f32[2,16,128]{2,1,0:T(8,128)} %fusion.63), channel_id=1, source_target_pairs={{0,2},{2,4},{4,6},{6,8},{8,10},{10,12},{12,14},{14,16},{16,18},{18... | collective-permute-start | bytes 49160 | tf_op jit(solution)/shard_map/ppermute | solution.py:21
  159.7 2.4 %collective-permute-start.22 = (f32[2,256]{1,0:T(2,128)S(1)}, f32[2,256]{1,0:T(2,128)}, u32[]{:S(2)}, u32[]{:S(2)}) collective-permute-start(f32[2,256]{1,0:T(2,128)S(1)} %reshape_squeeze.31), channel_id=1, source_target_pairs={{0,1},{2,3},{4,5},{6,7},{8,9},{10,11},{12,13},{14,15},{16,17},{18,... | collective-permute-start | bytes 6152 | tf_op jit(solution)/shard_map/ppermute | solution.py:21
  162.8 2.8 %collective-permute-start.23 = (f32[2,16,128]{2,1,0:T(8,128)}, f32[2,16,128]{2,1,0:T(8,128)S(1)}, u32[]{:S(2)}, u32[]{:S(2)}) collective-permute-start(f32[2,16,128]{2,1,0:T(8,128)} %bitcast.40), channel_id=1, source_target_pairs={{0,64},{64,128},{128,192},{1,65},{65,129},{129,193},{2,66},{66,130... | collective-permute-start | bytes 49160 | tf_op jit(solution)/shard_map/ppermute | solution.py:21
  166.5 1.0 fusion.7
  167.5 1.2 collective-permute-done.23
  168.9 1.9 %fusion.6 = (f32[3,16,16,128]{3,2,1,0:T(8,128)}, f32[3,16,16,128]{3,2,1,0:T(8,128)S(1)}) fusion(f32[1,16,16,128]{3,2,1,0:T(8,128)S(1)} %get-tuple-element.64, f32[1,16,16,128]{3,2,1,0:T(8,128)S(1)} %get-tuple-element.65, f32[1,16,16,128]{3,2,1,0:T(8,128)S(1)} %get-tuple-element.63, f32[16,16,128]{2,1,0:T(8,128)} %get-tuple-element.30, ...), kind=kLoop, calls=%fused_computation.26 | loop fusion | flops 1867776 | bytes 3145728 | tf_op jit(solution)/shard_map/sub | solution.py:112
  170.7 0.9 fusion.37
  172.2 1.9 %reduce.24 = f32[128,256]{1,0:T(8,128)S(1)} reduce(f32[128,1,256]{2,1,0:T(1,128)} %all-to-all-done, f32[]{:T(128)} %broadcast.190), dimensions={1}, to_apply=%all_to_all.12.reduce_sub_computation | reduce | bytes 262148 | tf_op jit(solution)/shard_map/all_to_all | solution.py:149
  174.2 1.8 fusion.24
  (156 shorter events, 33.8 us)
Async XLA Ops:
  0.6 44.6 %copy-start.2 = (f32[3,16,16,128]{3,2,1,0:T(8,128)S(1)}, f32[3,16,16,128]{3,2,1,0:T(8,128)}, u32[]{:S(2)}) copy-start(f32[3,16,16,128]{3,2,1,0:T(8,128)} %param.15) | copy-start | bytes 1179652
  1.7 40.9 %collective-permute-start = (f32[2,16,128]{2,1,0:T(8,128)S(1)}, f32[2,16,128]{2,1,0:T(8,128)S(1)}, u32[]{:S(2)}, u32[]{:S(2)}) collective-permute-start(f32[2,16,128]{2,1,0:T(8,128)S(1)} %fusion.57), channel_id=1, source_target_pairs={{2,0},{4,2},{6,4},{8,6},{10,8},{12,10},{14,12},{16,14},{18,16},{20... | collective-permute-start | bytes 49160 | tf_op jit(solution)/shard_map/ppermute | solution.py:21
  4.1 54.3 %copy-start = (f32[3,16,16,128]{3,2,1,0:T(8,128)S(1)}, f32[3,16,16,128]{3,2,1,0:T(8,128)}, u32[]{:S(2)}) copy-start(f32[3,16,16,128]{3,2,1,0:T(8,128)} %param.14) | copy-start | bytes 1179652
  4.1 54.3 %copy-start.1 = (f32[3,16,16,128]{3,2,1,0:T(8,128)S(1)}, f32[3,16,16,128]{3,2,1,0:T(8,128)}, u32[]{:S(2)}) copy-start(f32[3,16,16,128]{3,2,1,0:T(8,128)} %param.17) | copy-start | bytes 1179652
  4.1 54.3 %copy-start.3 = (f32[3,16,16,128]{3,2,1,0:T(8,128)S(1)}, f32[3,16,16,128]{3,2,1,0:T(8,128)}, u32[]{:S(2)}) copy-start(f32[3,16,16,128]{3,2,1,0:T(8,128)} %param.16) | copy-start | bytes 1179652
  4.2 34.6 %collective-permute-start.1 = (f32[2,256]{1,0:T(2,128)S(1)}, f32[2,256]{1,0:T(2,128)S(1)}, u32[]{:S(2)}, u32[]{:S(2)}) collective-permute-start(f32[2,256]{1,0:T(2,128)S(1)} %reshape_squeeze.24), channel_id=1, source_target_pairs={{1,0},{3,2},{5,4},{7,6},{9,8},{11,10},{13,12},{15,14},{17,16},{19,... | collective-permute-start | bytes 6152 | tf_op jit(solution)/shard_map/ppermute | solution.py:21
  6.5 36.1 %collective-permute-start.2 = (f32[2,16,128]{2,1,0:T(8,128)S(1)}, f32[2,16,128]{2,1,0:T(8,128)S(1)}, u32[]{:S(2)}, u32[]{:S(2)}) collective-permute-start(f32[2,16,128]{2,1,0:T(8,128)S(1)} %bitcast.135), channel_id=1, source_target_pairs={{64,0},{128,64},{192,128},{65,1},{129,65},{193,129},{66,2},{130,66... | collective-permute-start | bytes 49160 | tf_op jit(solution)/shard_map/ppermute | solution.py:21
  11.6 1.0 copy-start.14
  13.4 27.2 %all-to-all-start.1 = ((f32[1,128,4]{2,0,1:T(1,128)}), f32[1,128,4]{2,0,1:T(1,128)S(1)}, u32[]{:S(2)}, u32[]{:S(2)}) async-start(f32[1,128,4]{2,0,1:T(1,128)} %bitcast.57), calls=%async_computation.1 | async-start | bytes 131072 | tf_op jit(solution)/shard_map/all_to_all | solution.py:150
  32.6 6.3 %copy-start.13 = (pred[16,16,128]{2,1,0:T(8,128)(4,1)}, pred[16,16,128]{2,1,0:T(8,128)(4,1)S(1)}, u32[]{:S(2)}) copy-start(pred[16,16,128]{2,1,0:T(8,128)(4,1)S(1)} %get-tuple-element.31) | copy-start | bytes 98308
  44.6 0.6 copy-start.11
  47.1 9.3 %collective-permute-start.3 = (f32[2,16,128]{2,1,0:T(8,128)}, f32[2,16,128]{2,1,0:T(8,128)S(1)}, u32[]{:S(2)}, u32[]{:S(2)}) collective-permute-start(f32[2,16,128]{2,1,0:T(8,128)} %fusion.58), channel_id=1, source_target_pairs={{0,2},{2,4},{4,6},{6,8},{8,10},{10,12},{12,14},{14,16},{16,18},{18... | collective-permute-start | bytes 49160 | tf_op jit(solution)/shard_map/ppermute | solution.py:21
  49.8 5.7 %collective-permute-start.4 = (f32[2,256]{1,0:T(2,128)S(1)}, f32[2,256]{1,0:T(2,128)}, u32[]{:S(2)}, u32[]{:S(2)}) collective-permute-start(f32[2,256]{1,0:T(2,128)S(1)} %reshape_squeeze.25), channel_id=1, source_target_pairs={{0,1},{2,3},{4,5},{6,7},{8,9},{10,11},{12,13},{14,15},{16,17},{18,... | collective-permute-start | bytes 6152 | tf_op jit(solution)/shard_map/ppermute | solution.py:21
  52.4 5.8 %collective-permute-start.5 = (f32[2,16,128]{2,1,0:T(8,128)}, f32[2,16,128]{2,1,0:T(8,128)S(1)}, u32[]{:S(2)}, u32[]{:S(2)}) collective-permute-start(f32[2,16,128]{2,1,0:T(8,128)} %bitcast.8), channel_id=1, source_target_pairs={{0,64},{64,128},{128,192},{1,65},{65,129},{129,193},{2,66},{66,130... | collective-permute-start | bytes 49160 | tf_op jit(solution)/shard_map/ppermute | solution.py:21
  58.4 1.2 copy-start.4
  60.6 17.1 %collective-permute-start.6 = (f32[2,16,128]{2,1,0:T(8,128)S(1)}, f32[2,16,128]{2,1,0:T(8,128)S(1)}, u32[]{:S(2)}, u32[]{:S(2)}) collective-permute-start(f32[2,16,128]{2,1,0:T(8,128)S(1)} %fusion.59), channel_id=1, source_target_pairs={{2,0},{4,2},{6,4},{8,6},{10,8},{12,10},{14,12},{16,14},{18,16},{20... | collective-permute-start | bytes 49160 | tf_op jit(solution)/shard_map/ppermute | solution.py:21
  62.0 12.0 %collective-permute-start.7 = (f32[2,256]{1,0:T(2,128)S(1)}, f32[2,256]{1,0:T(2,128)S(1)}, u32[]{:S(2)}, u32[]{:S(2)}) collective-permute-start(f32[2,256]{1,0:T(2,128)S(1)} %reshape_squeeze.26), channel_id=1, source_target_pairs={{1,0},{3,2},{5,4},{7,6},{9,8},{11,10},{13,12},{15,14},{17,16},{19,... | collective-permute-start | bytes 6152 | tf_op jit(solution)/shard_map/ppermute | solution.py:21
  63.3 13.5 %collective-permute-start.13 = (f32[2,256]{1,0:T(2,128)S(1)}, f32[2,256]{1,0:T(2,128)S(1)}, u32[]{:S(2)}, u32[]{:S(2)}) collective-permute-start(f32[2,256]{1,0:T(2,128)S(1)} %reshape_squeeze.28), channel_id=1, source_target_pairs={{1,0},{3,2},{5,4},{7,6},{9,8},{11,10},{13,12},{15,14},{17,16},{19,... | collective-permute-start | bytes 6152 | tf_op jit(solution)/shard_map/ppermute | solution.py:21
  69.7 9.0 %collective-permute-start.8 = (f32[2,16,128]{2,1,0:T(8,128)S(1)}, f32[2,16,128]{2,1,0:T(8,128)S(1)}, u32[]{:S(2)}, u32[]{:S(2)}) collective-permute-start(f32[2,16,128]{2,1,0:T(8,128)S(1)} %bitcast.136), channel_id=1, source_target_pairs={{64,0},{128,64},{192,128},{65,1},{129,65},{193,129},{66,2},{130,66... | collective-permute-start | bytes 49160 | tf_op jit(solution)/shard_map/ppermute | solution.py:21
  72.7 9.5 %collective-permute-start.12 = (f32[2,16,128]{2,1,0:T(8,128)}, f32[2,16,128]{2,1,0:T(8,128)}, u32[]{:S(2)}, u32[]{:S(2)}) collective-permute-start(f32[2,16,128]{2,1,0:T(8,128)} %fusion.61), channel_id=1, source_target_pairs={{2,0},{4,2},{6,4},{8,6},{10,8},{12,10},{14,12},{16,14},{18,16},{20... | collective-permute-start | bytes 49160 | tf_op jit(solution)/shard_map/ppermute | solution.py:21
  74.0 9.2 %collective-permute-start.14 = (f32[2,16,128]{2,1,0:T(8,128)}, f32[2,16,128]{2,1,0:T(8,128)S(1)}, u32[]{:S(2)}, u32[]{:S(2)}) collective-permute-start(f32[2,16,128]{2,1,0:T(8,128)} %bitcast.25), channel_id=1, source_target_pairs={{64,0},{128,64},{192,128},{65,1},{129,65},{193,129},{66,2},{130,66... | collective-permute-start | bytes 49160 | tf_op jit(solution)/shard_map/ppermute | solution.py:21
  86.2 21.6 %collective-permute-start.9 = (f32[2,16,128]{2,1,0:T(8,128)S(1)}, f32[2,16,128]{2,1,0:T(8,128)S(1)}, u32[]{:S(2)}, u32[]{:S(2)}) collective-permute-start(f32[2,16,128]{2,1,0:T(8,128)S(1)} %fusion.60), channel_id=1, source_target_pairs={{0,2},{2,4},{4,6},{6,8},{8,10},{10,12},{12,14},{14,16},{16,18},{18... | collective-permute-start | bytes 49160 | tf_op jit(solution)/shard_map/ppermute | solution.py:21
  91.5 10.9 %collective-permute-start.10 = (f32[2,256]{1,0:T(2,128)S(1)}, f32[2,256]{1,0:T(2,128)S(1)}, u32[]{:S(2)}, u32[]{:S(2)}) collective-permute-start(f32[2,256]{1,0:T(2,128)S(1)} %reshape_squeeze.27), channel_id=1, source_target_pairs={{0,1},{2,3},{4,5},{6,7},{8,9},{10,11},{12,13},{14,15},{16,17},{18,... | collective-permute-start | bytes 6152 | tf_op jit(solution)/shard_map/ppermute | solution.py:21
  94.0 12.9 %collective-permute-start.16 = (f32[2,256]{1,0:T(2,128)S(1)}, f32[2,256]{1,0:T(2,128)S(1)}, u32[]{:S(2)}, u32[]{:S(2)}) collective-permute-start(f32[2,256]{1,0:T(2,128)S(1)} %reshape_squeeze.29), channel_id=1, source_target_pairs={{0,1},{2,3},{4,5},{6,7},{8,9},{10,11},{12,13},{14,15},{16,17},{18,... | collective-permute-start | bytes 6152 | tf_op jit(solution)/shard_map/ppermute | solution.py:21
  96.8 12.0 %collective-permute-start.11 = (f32[2,16,128]{2,1,0:T(8,128)S(1)}, f32[2,16,128]{2,1,0:T(8,128)S(1)}, u32[]{:S(2)}, u32[]{:S(2)}) collective-permute-start(f32[2,16,128]{2,1,0:T(8,128)S(1)} %bitcast.137), channel_id=1, source_target_pairs={{0,64},{64,128},{128,192},{1,65},{65,129},{129,193},{2,66},{66,130... | collective-permute-start | bytes 49160 | tf_op jit(solution)/shard_map/ppermute | solution.py:21
  100.4 9.7 %collective-permute-start.17 = (f32[2,16,128]{2,1,0:T(8,128)S(1)}, f32[2,16,128]{2,1,0:T(8,128)S(1)}, u32[]{:S(2)}, u32[]{:S(2)}) collective-permute-start(f32[2,16,128]{2,1,0:T(8,128)S(1)} %bitcast.129), channel_id=1, source_target_pairs={{0,64},{64,128},{128,192},{1,65},{65,129},{129,193},{2,66},{66,130... | collective-permute-start | bytes 49160 | tf_op jit(solution)/shard_map/ppermute | solution.py:21
  102.4 7.8 %collective-permute-start.15 = (f32[2,16,128]{2,1,0:T(8,128)S(1)}, f32[2,16,128]{2,1,0:T(8,128)S(1)}, u32[]{:S(2)}, u32[]{:S(2)}) collective-permute-start(f32[2,16,128]{2,1,0:T(8,128)S(1)} %fusion.56), channel_id=1, source_target_pairs={{0,2},{2,4},{4,6},{6,8},{8,10},{10,12},{12,14},{14,16},{16,18},{18... | collective-permute-start | bytes 49160 | tf_op jit(solution)/shard_map/ppermute | solution.py:21
  111.5 1.3 copy-start.5
  111.5 1.3 copy-start.7
  111.5 1.3 copy-start.9
  114.7 36.4 %collective-permute-start.18 = (f32[2,16,128]{2,1,0:T(8,128)}, f32[2,16,128]{2,1,0:T(8,128)S(1)}, u32[]{:S(2)}, u32[]{:S(2)}) collective-permute-start(f32[2,16,128]{2,1,0:T(8,128)} %fusion.62), channel_id=1, source_target_pairs={{2,0},{4,2},{6,4},{8,6},{10,8},{12,10},{14,12},{16,14},{18,16},{20... | collective-permute-start | bytes 49160 | tf_op jit(solution)/shard_map/ppermute | solution.py:21
  116.7 32.9 %collective-permute-start.19 = (f32[2,256]{1,0:T(2,128)}, f32[2,256]{1,0:T(2,128)}, u32[]{:S(2)}, u32[]{:S(2)}) collective-permute-start(f32[2,256]{1,0:T(2,128)} %reshape_squeeze.30), channel_id=1, source_target_pairs={{1,0},{3,2},{5,4},{7,6},{9,8},{11,10},{13,12},{15,14},{17,16},{19,... | collective-permute-start | bytes 6152 | tf_op jit(solution)/shard_map/ppermute | solution.py:21
  124.9 44.0 %copy-start.6 = (f32[1,16,16,128]{3,2,1,0:T(8,128)S(1)}, f32[1,16,16,128]{3,2,1,0:T(8,128)}, u32[]{:S(2)}) copy-start(f32[1,16,16,128]{3,2,1,0:T(8,128)} %copy-done.5) | copy-start | bytes 393220
  124.9 44.0 %copy-start.8 = (f32[1,16,16,128]{3,2,1,0:T(8,128)S(1)}, f32[1,16,16,128]{3,2,1,0:T(8,128)}, u32[]{:S(2)}) copy-start(f32[1,16,16,128]{3,2,1,0:T(8,128)} %copy-done.7) | copy-start | bytes 393220
  124.9 44.0 %copy-start.10 = (f32[1,16,16,128]{3,2,1,0:T(8,128)S(1)}, f32[1,16,16,128]{3,2,1,0:T(8,128)}, u32[]{:S(2)}) copy-start(f32[1,16,16,128]{3,2,1,0:T(8,128)} %copy-done.9) | copy-start | bytes 393220
  130.3 41.4 %all-to-all-start = ((f32[128,1,256]{2,1,0:T(1,128)}), f32[128,1,256]{2,1,0:T(1,128)}, u32[]{:S(2)}, u32[]{:S(2)}) async-start(f32[128,1,256]{2,1,0:T(1,128)} %reshape.198), calls=%async_computation | async-start | bytes 262144 | tf_op jit(solution)/shard_map/all_to_all | solution.py:149
  147.3 6.2 %collective-permute-start.20 = (f32[2,16,128]{2,1,0:T(8,128)}, f32[2,16,128]{2,1,0:T(8,128)S(1)}, u32[]{:S(2)}, u32[]{:S(2)}) collective-permute-start(f32[2,16,128]{2,1,0:T(8,128)} %bitcast.138), channel_id=1, source_target_pairs={{64,0},{128,64},{192,128},{65,1},{129,65},{193,129},{66,2},{130,66... | collective-permute-start | bytes 49160 | tf_op jit(solution)/shard_map/ppermute | solution.py:21
  156.2 10.2 %collective-permute-start.21 = (f32[2,16,128]{2,1,0:T(8,128)}, f32[2,16,128]{2,1,0:T(8,128)S(1)}, u32[]{:S(2)}, u32[]{:S(2)}) collective-permute-start(f32[2,16,128]{2,1,0:T(8,128)} %fusion.63), channel_id=1, source_target_pairs={{0,2},{2,4},{4,6},{6,8},{8,10},{10,12},{12,14},{14,16},{16,18},{18... | collective-permute-start | bytes 49160 | tf_op jit(solution)/shard_map/ppermute | solution.py:21
  159.7 5.9 %collective-permute-start.22 = (f32[2,256]{1,0:T(2,128)S(1)}, f32[2,256]{1,0:T(2,128)}, u32[]{:S(2)}, u32[]{:S(2)}) collective-permute-start(f32[2,256]{1,0:T(2,128)S(1)} %reshape_squeeze.31), channel_id=1, source_target_pairs={{0,1},{2,3},{4,5},{6,7},{8,9},{10,11},{12,13},{14,15},{16,17},{18,... | collective-permute-start | bytes 6152 | tf_op jit(solution)/shard_map/ppermute | solution.py:21
  162.8 5.8 %collective-permute-start.23 = (f32[2,16,128]{2,1,0:T(8,128)}, f32[2,16,128]{2,1,0:T(8,128)S(1)}, u32[]{:S(2)}, u32[]{:S(2)}) collective-permute-start(f32[2,16,128]{2,1,0:T(8,128)} %bitcast.40), channel_id=1, source_target_pairs={{0,64},{64,128},{128,192},{1,65},{65,129},{129,193},{2,66},{66,130... | collective-permute-start | bytes 49160 | tf_op jit(solution)/shard_map/ppermute | solution.py:21
  171.6 4.4 %copy-start.12 = (f32[3,16,16,128]{3,2,1,0:T(8,128)}, f32[3,16,16,128]{3,2,1,0:T(8,128)S(1)}, u32[]{:S(2)}) copy-start(f32[3,16,16,128]{3,2,1,0:T(8,128)S(1)} %fusion.37) | copy-start | bytes 1179652
where the time goes:
time: 178 us; the launch traced here: 176 us
  starting transfers between devices  88.3 us (50%)
  other arithmetic  41.9 us (24%)
  local copies, waits for them, and re-layouts  28.3 us (16%)
  matrix products  10 us (6%)
  waiting for transfers between devices  5.8 us (3%)
    ppermute x24, starting transfers between devices, passed_along(): return lax.ppermute(x, axis, pairs)  54.4 us
    all_to_all x1, starting transfers between devices, local(): lax.all_to_all(send_vals, ('bx', 'by'), split_axis=1, concat_axis=1, tile...  17 us
    all_to_all x1, starting transfers between devices, local(): lax.all_to_all(send_ids, ('bx', 'by'), split_axis=1, concat_axis=1, tiled...  16.9 us
    sub x8, other arithmetic, differ(): return neighbour - couple  7.75 us
    another operation x8, local copies, waits for them, and re-layouts, beside(): arrived = jnp.expand_dims(arrived, axis_dim)  7.18 us
    dot_general x1, matrix products, local(): jnp.einsum('tfkc,tc->tfk', blocks, cell_tiles, preferred_element_type=jnp...  6.71 us
    slice x8, local copies, waits for them, and re-layouts, beside(): lax.slice_in_dim(couple, 1, length, axis=axis_dim)  5.3 us
    slice x13, local copies, waits for them, and re-layouts, beside(): lax.index_in_dim(couple, border_at, axis=axis_dim, keepdims=False)  5.01 us
  transfers between devices with their start and end apart: 26, of which 4 were waited for; matrix products, arithmetic and copies ran while one was open for 34% of the time, Pallas kernels for 0%

commit v1 on v0

--- a/solution.py
+++ b/solution.py
@@ -146,7 +146,15 @@
         - 1.0
     )
     got_vals, got_ids = (
-        lax.all_to_all(send_vals, ("bx", "by"), split_axis=1, concat_axis=1, tiled=True),
+        jnp.concatenate(
+            lax.all_to_all(
+                jnp.stack(jnp.split(send_vals, lax.axis_size(("bx", "by")), axis=1)),
+                axis_name=("bx", "by"),
+                split_axis=0,
+                concat_axis=0,
+            ),
+            axis=1,
+        ),
         lax.all_to_all(send_ids, ("bx", "by"), split_axis=1, concat_axis=1, tiled=True),
     )
     group_hits = (

time: 178 us -> 269 us (1.51)
  local copies, waits for them, and re-layouts: 28.3 us -> 120 us
    unnamed x33 -> x172, local copies, waits for them, and re-layouts: 2.72 us -> 88.8 us
    ppermute x24, starting transfers between devices: 54.4 us -> 59.4 us  [passed_along(): return lax.ppermute(x, axis, pairs)]
    another operation x4 -> x6, local copies, waits for them, and re-layouts: 0.02 us -> 4.31 us  [the longest x2 4.29 us: local(): jnp.stack(jnp.split(send_vals, lax.axis_size(('bx', 'by')), axis=1))]
    all_to_all x1, starting transfers between devices: 17 us -> 14.2 us  [local(): lax.all_to_all(jnp.stack(jnp.split(send_vals, lax.axis_size(('bx', 'by'))...]
  transfers between devices with their start and end apart: 26 -> 26, of which waited for: 4 -> 3; matrix products, arithmetic and copies ran while one was open for 34% -> 57% of each run, Pallas kernels for 0% -> 0%
where the time goes in v1:
time: 269 us; the launch traced here: 267 us
  local copies, waits for them, and re-layouts  120 us (45%)
  starting transfers between devices  90.6 us (34%)
  other arithmetic  39.5 us (15%)
  matrix products  9.19 us (3%)
  waiting for transfers between devices  5.85 us (2%)
    unnamed x172, local copies, waits for them, and re-layouts  88.8 us
    ppermute x24, starting transfers between devices, passed_along(): return lax.ppermute(x, axis, pairs)  59.4 us
    all_to_all x1, starting transfers between devices, local(): lax.all_to_all(send_ids, ('bx', 'by'), split_axis=1, concat_axis=1, tiled...  16.9 us
    all_to_all x1, starting transfers between devices, local(): lax.all_to_all(jnp.stack(jnp.split(send_vals, lax.axis_size(('bx', 'by'))...  14.2 us
    another operation x8, local copies, waits for them, and re-layouts, beside(): arrived = jnp.expand_dims(arrived, axis_dim)  7.73 us
    dot_general x1, matrix products, local(): jnp.einsum('tfkc,tc->tfk', blocks, cell_tiles, preferred_element_type=jnp...  6.71 us
    slice x13, local copies, waits for them, and re-layouts, beside(): lax.index_in_dim(couple, border_at, axis=axis_dim, keepdims=False)  6.27 us
    sub x8, other arithmetic, differ(): return neighbour - couple  6.24 us
  transfers between devices with their start and end apart: 26, of which 3 were waited for; matrix products, arithmetic and copies ran while one was open for 57% of the time, Pallas kernels for 0%

profile of v1, /device:TPU:4, one launch (start us, length us, event | category | flops | bytes accessed | tf_op | source)
XLA Modules:
  0.0 267.3 jit_solution(5432639141790778856)
XLA Ops:
  0.6 1.2 slice_reduce_fusion.6
  1.9 1.3 collective-permute-start.1
  3.2 0.9 slice.468
  4.1 2.4 collective-permute-start.2
  6.5 1.0 fusion.67
  7.5 1.3 collective-permute-start
  8.8 0.8 copy.237
  10.0 0.9 fusion.37
  12.6 0.8 all_to_all.10
  13.3 16.9 %all-to-all-start.1 = ((f32[1,128,4]{2,0,1:T(1,128)}), f32[1,128,4]{2,0,1:T(1,128)S(1)}, u32[]{:S(2)}, u32[]{:S(2)}) async-start(f32[1,128,4]{2,0,1:T(1,128)} %bitcast.185), calls=%async_computation.1 | async-start | bytes 131072 | tf_op jit(solution)/shard_map/all_to_all | solution.py:158
  30.3 1.6 broadcast_select_fusion
  33.9 1.6 fusion.40
  36.6 3.8 %all-to-all-done.1 = f32[1,128,4]{2,0,1:T(1,128)S(1)} async-done(((f32[1,128,4]{2,0,1:T(1,128)}), f32[1,128,4]{2,0,1:T(1,128)S(1)}, u32[]{:S(2)}, u32[]{:S(2)}) %all-to-all-start.1) | async-done | bytes 2080 | tf_op jit(solution)/shard_map/all_to_all | solution.py:158
  40.9 0.8 reduce.23
  43.6 1.8 collective-permute-start.4
  46.1 3.1 %collective-permute-start.3 = (f32[2,16,128]{2,1,0:T(8,128)}, f32[2,16,128]{2,1,0:T(8,128)}, u32[]{:S(2)}, u32[]{:S(2)}) collective-permute-start(f32[2,16,128]{2,1,0:T(8,128)} %fusion.56), channel_id=1, source_target_pairs={{0,2},{2,4},{4,6},{6,8},{8,10},{10,12},{12,14},{14,16},{16,18},{18... | collective-permute-start | bytes 49160 | tf_op jit(solution)/shard_map/ppermute | solution.py:21
  50.5 2.6 collective-permute-start.5
  53.1 0.8 broadcast_in_dim_reshape.33
  54.0 1.0 fusion.15
  55.0 1.3 collective-permute-done.5
  60.0 1.3 collective-permute-start.13
  61.3 1.3 collective-permute-start.12
  62.6 1.4 reshape_squeeze.26
  64.0 1.3 collective-permute-start.7
  66.6 0.8 slice.637
  68.8 0.8 slice.604
  70.9 3.0 %collective-permute-start.14 = (f32[2,16,128]{2,1,0:T(8,128)}, f32[2,16,128]{2,1,0:T(8,128)S(1)}, u32[]{:S(2)}, u32[]{:S(2)}) collective-permute-start(f32[2,16,128]{2,1,0:T(8,128)} %bitcast.25), channel_id=1, source_target_pairs={{64,0},{128,64},{192,128},{65,1},{129,65},{193,129},{66,2},{130,66... | collective-permute-start | bytes 49160 | tf_op jit(solution)/shard_map/ppermute | solution.py:21
  73.9 1.9 collective-permute-start.8
  75.9 1.3 collective-permute-start.6
  77.2 1.5 broadcast_in_dim_reshape.36
  78.7 1.6 broadcast_in_dim_reshape.34
  80.4 1.1 fusion.12
  81.5 1.3 slice_subtract_fusion.5
  87.2 0.9 slice_subtract_fusion.9
  88.6 3.8 %collective-permute-start.16 = (f32[2,256]{1,0:T(2,128)S(1)}, f32[2,256]{1,0:T(2,128)S(1)}, u32[]{:S(2)}, u32[]{:S(2)}) collective-permute-start(f32[2,256]{1,0:T(2,128)S(1)} %reshape_squeeze.29), channel_id=1, source_target_pairs={{0,1},{2,3},{4,5},{6,7},{8,9},{10,11},{12,13},{14,15},{16,17},{18,... | collective-permute-start | bytes 6152 | tf_op jit(solution)/shard_map/ppermute | solution.py:21
  92.5 4.9 %collective-permute-start.15 = (f32[2,16,128]{2,1,0:T(8,128)}, f32[2,16,128]{2,1,0:T(8,128)S(1)}, u32[]{:S(2)}, u32[]{:S(2)}) collective-permute-start(f32[2,16,128]{2,1,0:T(8,128)} %fusion.54), channel_id=1, source_target_pairs={{0,2},{2,4},{4,6},{6,8},{8,10},{10,12},{12,14},{14,16},{16,18},{18... | collective-permute-start | bytes 49160 | tf_op jit(solution)/shard_map/ppermute | solution.py:21
  97.4 4.2 %collective-permute-start.17 = (f32[2,16,128]{2,1,0:T(8,128)}, f32[2,16,128]{2,1,0:T(8,128)S(1)}, u32[]{:S(2)}, u32[]{:S(2)}) collective-permute-start(f32[2,16,128]{2,1,0:T(8,128)} %bitcast.639), channel_id=1, source_target_pairs={{0,64},{64,128},{128,192},{1,65},{65,129},{129,193},{2,66},{66,130... | collective-permute-start | bytes 49160 | tf_op jit(solution)/shard_map/ppermute | solution.py:21
  101.7 1.3 collective-permute-start.10
  105.1 1.9 collective-permute-start.11
  107.1 3.6 %collective-permute-start.9 = (f32[2,16,128]{2,1,0:T(8,128)S(1)}, f32[2,16,128]{2,1,0:T(8,128)S(1)}, u32[]{:S(2)}, u32[]{:S(2)}) collective-permute-start(f32[2,16,128]{2,1,0:T(8,128)S(1)} %fusion.58), channel_id=1, source_target_pairs={{0,2},{2,4},{4,6},{6,8},{8,10},{10,12},{12,14},{14,16},{16,18},{18... | collective-permute-start | bytes 49160 | tf_op jit(solution)/shard_map/ppermute | solution.py:21
  110.9 0.9 broadcast_in_dim_reshape.35
  111.9 1.4 fusion.17
  113.3 1.0 fusion.13
  114.5 1.9 multiply_reduce_fusion.1
  119.4 1.3 collective-permute-start.19
  120.7 3.9 %collective-permute-start.20 = (f32[2,16,128]{2,1,0:T(8,128)}, f32[2,16,128]{2,1,0:T(8,128)S(1)}, u32[]{:S(2)}, u32[]{:S(2)}) collective-permute-start(f32[2,16,128]{2,1,0:T(8,128)} %bitcast.35), channel_id=1, source_target_pairs={{64,0},{128,64},{192,128},{65,1},{129,65},{193,129},{66,2},{130,66... | collective-permute-start | bytes 49160 | tf_op jit(solution)/shard_map/ppermute | solution.py:21
  124.6 1.5 collective-permute-start.18
  126.1 1.8 fusion.33
  127.9 0.9 reshape.165
  128.8 6.7 %fusion.68 = f32[128,1,2,64]{3,1,2,0:T(1,128)S(1)} fusion(bf16[128,256,1,1]{1,2,3,0:T(2,128)(2,1)S(1)} %reshape.165, bf16[128,2,64,256]{3,2,1,0:T(8,128)(2,1)} %bitcast.622), kind=kOutput, calls=%fused_computation.457 | convolution fusion | flops 8388608 | bytes 8519680 | tf_op jit(solution)/shard_map/tfkc,tc->tfk/dot_general | solution.py:123
  222.6 3.6 %copy.239 = f32[128,64,4]{1,2,0:T(4,128)} copy(f32[128,64,4]{2,1,0:T(8,128)} %constant_dynamic-update-slice_fusion) | data formatting | bytes 262144 | tf_op jit(solution)/shard_map/stack | solution.py:151
  226.2 1.8 reshape.185
  228.0 14.2 %all-to-all-start = ((f32[128,1,256]{2,1,0:T(1,128)}), f32[128,1,256]{2,1,0:T(1,128)}, u32[]{:S(2)}, u32[]{:S(2)}) async-start(f32[128,1,256]{2,1,0:T(1,128)} %reshape.185), calls=%async_computation | async-start | bytes 262144 | tf_op jit(solution)/shard_map/all_to_all | solution.py:150
  242.3 1.6 broadcast_in_dim_reshape.38
  243.8 1.0 fusion.7
  244.9 1.1 slice_subtract_fusion.3
  247.2 3.0 %collective-permute-start.22 = (f32[2,256]{1,0:T(2,128)S(1)}, f32[2,256]{1,0:T(2,128)}, u32[]{:S(2)}, u32[]{:S(2)}) collective-permute-start(f32[2,256]{1,0:T(2,128)S(1)} %reshape_squeeze.31), channel_id=1, source_target_pairs={{0,1},{2,3},{4,5},{6,7},{8,9},{10,11},{12,13},{14,15},{16,17},{18,... | collective-permute-start | bytes 6152 | tf_op jit(solution)/shard_map/ppermute | solution.py:21
  250.2 4.0 %collective-permute-start.21 = (f32[2,16,128]{2,1,0:T(8,128)S(1)}, f32[2,16,128]{2,1,0:T(8,128)}, u32[]{:S(2)}, u32[]{:S(2)}) collective-permute-start(f32[2,16,128]{2,1,0:T(8,128)S(1)} %fusion.61), channel_id=1, source_target_pairs={{0,2},{2,4},{4,6},{6,8},{8,10},{10,12},{12,14},{14,16},{16,18},{18... | collective-permute-start | bytes 49160 | tf_op jit(solution)/shard_map/ppermute | solution.py:21
  254.8 3.4 %collective-permute-start.23 = (f32[2,16,128]{2,1,0:T(8,128)}, f32[2,16,128]{2,1,0:T(8,128)S(1)}, u32[]{:S(2)}, u32[]{:S(2)}) collective-permute-start(f32[2,16,128]{2,1,0:T(8,128)} %bitcast.40), channel_id=1, source_target_pairs={{0,64},{64,128},{128,192},{1,65},{65,129},{129,193},{2,66},{66,130... | collective-permute-start | bytes 49160 | tf_op jit(solution)/shard_map/ppermute | solution.py:21
  258.2 0.8 broadcast_in_dim_reshape.39
  259.1 1.0 fusion.6
  261.0 1.9 fusion.5
  263.5 1.9 reduce.24
  265.5 1.8 fusion.22
  (295 shorter events, 118.1 us)
Async XLA Ops:
  0.6 35.6 %copy-start = (f32[3,16,16,128]{3,2,1,0:T(8,128)S(1)}, f32[3,16,16,128]{3,2,1,0:T(8,128)}, u32[]{:S(2)}) copy-start(f32[3,16,16,128]{3,2,1,0:T(8,128)} %param.14) | copy-start | bytes 1179652
  1.9 34.5 %collective-permute-start.1 = (f32[2,256]{1,0:T(2,128)S(1)}, f32[2,256]{1,0:T(2,128)S(1)}, u32[]{:S(2)}, u32[]{:S(2)}) collective-permute-start(f32[2,256]{1,0:T(2,128)S(1)} %reshape_squeeze.24), channel_id=1, source_target_pairs={{1,0},{3,2},{5,4},{7,6},{9,8},{11,10},{13,12},{15,14},{17,16},{19,... | collective-permute-start | bytes 6152 | tf_op jit(solution)/shard_map/ppermute | solution.py:21
  4.1 38.3 %collective-permute-start.2 = (f32[2,16,128]{2,1,0:T(8,128)S(1)}, f32[2,16,128]{2,1,0:T(8,128)S(1)}, u32[]{:S(2)}, u32[]{:S(2)}) collective-permute-start(f32[2,16,128]{2,1,0:T(8,128)S(1)} %bitcast.642), channel_id=1, source_target_pairs={{64,0},{128,64},{192,128},{65,1},{129,65},{193,129},{66,2},{130,66... | collective-permute-start | bytes 49160 | tf_op jit(solution)/shard_map/ppermute | solution.py:21
  7.5 34.8 %collective-permute-start = (f32[2,16,128]{2,1,0:T(8,128)S(1)}, f32[2,16,128]{2,1,0:T(8,128)S(1)}, u32[]{:S(2)}, u32[]{:S(2)}) collective-permute-start(f32[2,16,128]{2,1,0:T(8,128)S(1)} %fusion.55), channel_id=1, source_target_pairs={{2,0},{4,2},{6,4},{8,6},{10,8},{12,10},{14,12},{16,14},{18,16},{20... | collective-permute-start | bytes 49160 | tf_op jit(solution)/shard_map/ppermute | solution.py:21
  9.8 32.8 %copy-start.2 = (f32[3,16,16,128]{3,2,1,0:T(8,128)S(1)}, f32[3,16,16,128]{3,2,1,0:T(8,128)}, u32[]{:S(2)}) copy-start(f32[3,16,16,128]{3,2,1,0:T(8,128)} %param.15) | copy-start | bytes 1179652
  11.5 1.0 copy-start.19
  13.3 27.0 %all-to-all-start.1 = ((f32[1,128,4]{2,0,1:T(1,128)}), f32[1,128,4]{2,0,1:T(1,128)S(1)}, u32[]{:S(2)}, u32[]{:S(2)}) async-start(f32[1,128,4]{2,0,1:T(1,128)} %bitcast.185), calls=%async_computation.1 | async-start | bytes 131072 | tf_op jit(solution)/shard_map/all_to_all | solution.py:158
  31.9 4.3 %copy-start.16 = (pred[16,16,128]{2,1,0:T(8,128)(4,1)}, pred[16,16,128]{2,1,0:T(8,128)(4,1)S(1)}, u32[]{:S(2)}) copy-start(pred[16,16,128]{2,1,0:T(8,128)(4,1)S(1)} %get-tuple-element.31) | copy-start | bytes 98308
  42.6 0.7 copy-start.6
  42.6 14.0 %copy-start.1 = (f32[3,16,16,128]{3,2,1,0:T(8,128)S(1)}, f32[3,16,16,128]{3,2,1,0:T(8,128)}, u32[]{:S(2)}) copy-start(f32[3,16,16,128]{3,2,1,0:T(8,128)} %param.17) | copy-start | bytes 1179652
  42.6 14.0 %copy-start.3 = (f32[3,16,16,128]{3,2,1,0:T(8,128)S(1)}, f32[3,16,16,128]{3,2,1,0:T(8,128)}, u32[]{:S(2)}) copy-start(f32[3,16,16,128]{3,2,1,0:T(8,128)} %param.16) | copy-start | bytes 1179652
  43.6 9.5 %collective-permute-start.4 = (f32[2,256]{1,0:T(2,128)S(1)}, f32[2,256]{1,0:T(2,128)}, u32[]{:S(2)}, u32[]{:S(2)}) collective-permute-start(f32[2,256]{1,0:T(2,128)S(1)} %reshape_squeeze.25), channel_id=1, source_target_pairs={{0,1},{2,3},{4,5},{6,7},{8,9},{10,11},{12,13},{14,15},{16,17},{18,... | collective-permute-start | bytes 6152 | tf_op jit(solution)/shard_map/ppermute | solution.py:21
  46.1 7.9 %collective-permute-start.3 = (f32[2,16,128]{2,1,0:T(8,128)}, f32[2,16,128]{2,1,0:T(8,128)}, u32[]{:S(2)}, u32[]{:S(2)}) collective-permute-start(f32[2,16,128]{2,1,0:T(8,128)} %fusion.56), channel_id=1, source_target_pairs={{0,2},{2,4},{4,6},{6,8},{8,10},{10,12},{12,14},{14,16},{16,18},{18... | collective-permute-start | bytes 49160 | tf_op jit(solution)/shard_map/ppermute | solution.py:21
  50.5 5.8 %collective-permute-start.5 = (f32[2,16,128]{2,1,0:T(8,128)}, f32[2,16,128]{2,1,0:T(8,128)S(1)}, u32[]{:S(2)}, u32[]{:S(2)}) collective-permute-start(f32[2,16,128]{2,1,0:T(8,128)} %bitcast.8), channel_id=1, source_target_pairs={{0,64},{64,128},{128,192},{1,65},{65,129},{129,193},{2,66},{66,130... | collective-permute-start | bytes 49160 | tf_op jit(solution)/shard_map/ppermute | solution.py:21
  54.0 3.3 %copy-start.18 = (f32[32768]{0:T(1024)S(1)}, f32[32768]{0:T(1024)}, u32[]{:S(2)}) copy-start(f32[32768]{0:T(1024)} %get-tuple-element.90) | copy-start | bytes 393220
  56.6 0.7 copy-start.4
  56.6 2.0 copy-start.5
  60.0 15.9 %collective-permute-start.13 = (f32[2,256]{1,0:T(2,128)}, f32[2,256]{1,0:T(2,128)}, u32[]{:S(2)}, u32[]{:S(2)}) collective-permute-start(f32[2,256]{1,0:T(2,128)} %reshape_squeeze.28), channel_id=1, source_target_pairs={{1,0},{3,2},{5,4},{7,6},{9,8},{11,10},{13,12},{15,14},{17,16},{19,... | collective-permute-start | bytes 6152 | tf_op jit(solution)/shard_map/ppermute | solution.py:21
  61.3 19.0 %collective-permute-start.12 = (f32[2,16,128]{2,1,0:T(8,128)}, f32[2,16,128]{2,1,0:T(8,128)}, u32[]{:S(2)}, u32[]{:S(2)}) collective-permute-start(f32[2,16,128]{2,1,0:T(8,128)} %fusion.59), channel_id=1, source_target_pairs={{2,0},{4,2},{6,4},{8,6},{10,8},{12,10},{14,12},{16,14},{18,16},{20... | collective-permute-start | bytes 49160 | tf_op jit(solution)/shard_map/ppermute | solution.py:21
  64.0 14.8 %collective-permute-start.7 = (f32[2,256]{1,0:T(2,128)}, f32[2,256]{1,0:T(2,128)}, u32[]{:S(2)}, u32[]{:S(2)}) collective-permute-start(f32[2,256]{1,0:T(2,128)} %reshape_squeeze.26), channel_id=1, source_target_pairs={{1,0},{3,2},{5,4},{7,6},{9,8},{11,10},{13,12},{15,14},{17,16},{19,... | collective-permute-start | bytes 6152 | tf_op jit(solution)/shard_map/ppermute | solution.py:21
  70.9 10.5 %collective-permute-start.14 = (f32[2,16,128]{2,1,0:T(8,128)}, f32[2,16,128]{2,1,0:T(8,128)S(1)}, u32[]{:S(2)}, u32[]{:S(2)}) collective-permute-start(f32[2,16,128]{2,1,0:T(8,128)} %bitcast.25), channel_id=1, source_target_pairs={{64,0},{128,64},{192,128},{65,1},{129,65},{193,129},{66,2},{130,66... | collective-permute-start | bytes 49160 | tf_op jit(solution)/shard_map/ppermute | solution.py:21
  73.9 13.3 %collective-permute-start.8 = (f32[2,16,128]{2,1,0:T(8,128)}, f32[2,16,128]{2,1,0:T(8,128)}, u32[]{:S(2)}, u32[]{:S(2)}) collective-permute-start(f32[2,16,128]{2,1,0:T(8,128)} %bitcast.14), channel_id=1, source_target_pairs={{64,0},{128,64},{192,128},{65,1},{129,65},{193,129},{66,2},{130,66... | collective-permute-start | bytes 49160 | tf_op jit(solution)/shard_map/ppermute | solution.py:21
  75.9 9.7 %collective-permute-start.6 = (f32[2,16,128]{2,1,0:T(8,128)}, f32[2,16,128]{2,1,0:T(8,128)}, u32[]{:S(2)}, u32[]{:S(2)}) collective-permute-start(f32[2,16,128]{2,1,0:T(8,128)} %fusion.57), channel_id=1, source_target_pairs={{2,0},{4,2},{6,4},{8,6},{10,8},{12,10},{14,12},{16,14},{18,16},{20... | collective-permute-start | bytes 49160 | tf_op jit(solution)/shard_map/ppermute | solution.py:21
  80.3 5.3 %copy-start.14 = (f32[2,15,16,128]{3,2,1,0:T(8,128)S(1)}, f32[2,15,16,128]{3,2,1,0:T(8,128)}, u32[]{:S(2)}) copy-start(f32[2,15,16,128]{3,2,1,0:T(8,128)} %fusion.28) | copy-start | bytes 737284
  80.3 6.9 %copy-start.8 = (f32[2,16,16,127]{3,2,1,0:T(8,128)S(1)}, f32[2,16,16,127]{3,2,1,0:T(8,128)}, u32[]{:S(2)}) copy-start(f32[2,16,16,127]{3,2,1,0:T(8,128)} %slice.604) | copy-start | bytes 780292
  80.3 6.9 %copy-start.9 = (f32[2,16,15,128]{3,2,1,0:T(8,128)S(1)}, f32[2,16,15,128]{3,2,1,0:T(8,128)}, u32[]{:S(2)}) copy-start(f32[2,16,15,128]{3,2,1,0:T(8,128)} %slice.608) | copy-start | bytes 737284
  80.3 6.9 %copy-start.12 = (f32[2,16,16,1]{3,2,1,0:T(8,128)S(1)}, f32[2,16,16,1]{3,2,1,0:T(8,128)}, u32[]{:S(2)}) copy-start(f32[2,16,16,1]{3,2,1,0:T(8,128)} %broadcast_in_dim_reshape.34) | copy-start | bytes 6148
  81.5 6.7 %copy-start.7 = (f32[1,16,16,128]{3,2,1,0:T(8,128)S(1)}, f32[1,16,16,128]{3,2,1,0:T(8,128)}, u32[]{:S(2)}) copy-start(f32[1,16,16,128]{3,2,1,0:T(8,128)} %copy-done.6) | copy-start | bytes 393220
  88.6 18.4 %collective-permute-start.16 = (f32[2,256]{1,0:T(2,128)S(1)}, f32[2,256]{1,0:T(2,128)S(1)}, u32[]{:S(2)}, u32[]{:S(2)}) collective-permute-start(f32[2,256]{1,0:T(2,128)S(1)} %reshape_squeeze.29), channel_id=1, source_target_pairs={{0,1},{2,3},{4,5},{6,7},{8,9},{10,11},{12,13},{14,15},{16,17},{18,... | collective-permute-start | bytes 6152 | tf_op jit(solution)/shard_map/ppermute | solution.py:21
  92.5 19.4 %collective-permute-start.15 = (f32[2,16,128]{2,1,0:T(8,128)}, f32[2,16,128]{2,1,0:T(8,128)S(1)}, u32[]{:S(2)}, u32[]{:S(2)}) collective-permute-start(f32[2,16,128]{2,1,0:T(8,128)} %fusion.54), channel_id=1, source_target_pairs={{0,2},{2,4},{4,6},{6,8},{8,10},{10,12},{12,14},{14,16},{16,18},{18... | collective-permute-start | bytes 49160 | tf_op jit(solution)/shard_map/ppermute | solution.py:21
  97.4 14.5 %collective-permute-start.17 = (f32[2,16,128]{2,1,0:T(8,128)}, f32[2,16,128]{2,1,0:T(8,128)S(1)}, u32[]{:S(2)}, u32[]{:S(2)}) collective-permute-start(f32[2,16,128]{2,1,0:T(8,128)} %bitcast.639), channel_id=1, source_target_pairs={{0,64},{64,128},{128,192},{1,65},{65,129},{129,193},{2,66},{66,130... | collective-permute-start | bytes 49160 | tf_op jit(solution)/shard_map/ppermute | solution.py:21
  101.7 9.3 %collective-permute-start.10 = (f32[2,256]{1,0:T(2,128)S(1)}, f32[2,256]{1,0:T(2,128)S(1)}, u32[]{:S(2)}, u32[]{:S(2)}) collective-permute-start(f32[2,256]{1,0:T(2,128)S(1)} %reshape_squeeze.27), channel_id=1, source_target_pairs={{0,1},{2,3},{4,5},{6,7},{8,9},{10,11},{12,13},{14,15},{16,17},{18,... | collective-permute-start | bytes 6152 | tf_op jit(solution)/shard_map/ppermute | solution.py:21
  105.1 9.2 %collective-permute-start.11 = (f32[2,16,128]{2,1,0:T(8,128)S(1)}, f32[2,16,128]{2,1,0:T(8,128)S(1)}, u32[]{:S(2)}, u32[]{:S(2)}) collective-permute-start(f32[2,16,128]{2,1,0:T(8,128)S(1)} %bitcast.643), channel_id=1, source_target_pairs={{0,64},{64,128},{128,192},{1,65},{65,129},{129,193},{2,66},{66,130... | collective-permute-start | bytes 49160 | tf_op jit(solution)/shard_map/ppermute | solution.py:21
  107.1 6.2 %collective-permute-start.9 = (f32[2,16,128]{2,1,0:T(8,128)S(1)}, f32[2,16,128]{2,1,0:T(8,128)S(1)}, u32[]{:S(2)}, u32[]{:S(2)}) collective-permute-start(f32[2,16,128]{2,1,0:T(8,128)S(1)} %fusion.58), channel_id=1, source_target_pairs={{0,2},{2,4},{4,6},{6,8},{8,10},{10,12},{12,14},{14,16},{16,18},{18... | collective-permute-start | bytes 49160 | tf_op jit(solution)/shard_map/ppermute | solution.py:21
  111.8 2.5 copy-start.10
  111.9 2.5 copy-start.11
  111.9 2.5 copy-start.13
  119.4 122.8 %collective-permute-start.19 = (f32[2,256]{1,0:T(2,128)}, f32[2,256]{1,0:T(2,128)}, u32[]{:S(2)}, u32[]{:S(2)}) collective-permute-start(f32[2,256]{1,0:T(2,128)} %reshape_squeeze.30), channel_id=1, source_target_pairs={{1,0},{3,2},{5,4},{7,6},{9,8},{11,10},{13,12},{15,14},{17,16},{19,... | collective-permute-start | bytes 6152 | tf_op jit(solution)/shard_map/ppermute | solution.py:21
  120.7 124.1 %collective-permute-start.20 = (f32[2,16,128]{2,1,0:T(8,128)}, f32[2,16,128]{2,1,0:T(8,128)S(1)}, u32[]{:S(2)}, u32[]{:S(2)}) collective-permute-start(f32[2,16,128]{2,1,0:T(8,128)} %bitcast.35), channel_id=1, source_target_pairs={{64,0},{128,64},{192,128},{65,1},{129,65},{193,129},{66,2},{130,66... | collective-permute-start | bytes 49160 | tf_op jit(solution)/shard_map/ppermute | solution.py:21
  124.6 119.2 %collective-permute-start.18 = (f32[2,16,128]{2,1,0:T(8,128)}, f32[2,16,128]{2,1,0:T(8,128)}, u32[]{:S(2)}, u32[]{:S(2)}) collective-permute-start(f32[2,16,128]{2,1,0:T(8,128)} %fusion.60), channel_id=1, source_target_pairs={{2,0},{4,2},{6,4},{8,6},{10,8},{12,10},{14,12},{16,14},{18,16},{20... | collective-permute-start | bytes 49160 | tf_op jit(solution)/shard_map/ppermute | solution.py:21
  128.8 6.7 %copy-start.20 = (s32[256,1]{0,1:T(1,128)S(1)}, s32[256,1]{0,1:T(1,128)}, u32[]{:S(2)}) copy-start(s32[256,1]{0,1:T(1,128)} %copy-done.19) | copy-start | bytes 3076
  228.0 34.9 %all-to-all-start = ((f32[128,1,256]{2,1,0:T(1,128)}), f32[128,1,256]{2,1,0:T(1,128)}, u32[]{:S(2)}, u32[]{:S(2)}) async-start(f32[128,1,256]{2,1,0:T(1,128)} %reshape.185), calls=%async_computation | async-start | bytes 262144 | tf_op jit(solution)/shard_map/all_to_all | solution.py:150
  247.2 11.1 %collective-permute-start.22 = (f32[2,256]{1,0:T(2,128)S(1)}, f32[2,256]{1,0:T(2,128)}, u32[]{:S(2)}, u32[]{:S(2)}) collective-permute-start(f32[2,256]{1,0:T(2,128)S(1)} %reshape_squeeze.31), channel_id=1, source_target_pairs={{0,1},{2,3},{4,5},{6,7},{8,9},{10,11},{12,13},{14,15},{16,17},{18,... | collective-permute-start | bytes 6152 | tf_op jit(solution)/shard_map/ppermute | solution.py:21
  250.2 8.9 %collective-permute-start.21 = (f32[2,16,128]{2,1,0:T(8,128)S(1)}, f32[2,16,128]{2,1,0:T(8,128)}, u32[]{:S(2)}, u32[]{:S(2)}) collective-permute-start(f32[2,16,128]{2,1,0:T(8,128)S(1)} %fusion.61), channel_id=1, source_target_pairs={{0,2},{2,4},{4,6},{6,8},{8,10},{10,12},{12,14},{14,16},{16,18},{18... | collective-permute-start | bytes 49160 | tf_op jit(solution)/shard_map/ppermute | solution.py:21
  254.8 8.1 %copy-start.17 = (f32[32768]{0:T(1024)S(1)}, f32[32768]{0:T(1024)}, u32[]{:S(2)}) copy-start(f32[32768]{0:T(1024)} %get-tuple-element.89) | copy-start | bytes 393220
  254.8 6.0 %collective-permute-start.23 = (f32[2,16,128]{2,1,0:T(8,128)}, f32[2,16,128]{2,1,0:T(8,128)S(1)}, u32[]{:S(2)}, u32[]{:S(2)}) collective-permute-start(f32[2,16,128]{2,1,0:T(8,128)} %bitcast.40), channel_id=1, source_target_pairs={{0,64},{64,128},{128,192},{1,65},{65,129},{129,193},{2,66},{66,130... | collective-permute-start | bytes 49160 | tf_op jit(solution)/shard_map/ppermute | solution.py:21
  262.9 4.4 %copy-start.15 = (f32[3,16,16,128]{3,2,1,0:T(8,128)}, f32[3,16,16,128]{3,2,1,0:T(8,128)S(1)}, u32[]{:S(2)}) copy-start(f32[3,16,16,128]{3,2,1,0:T(8,128)S(1)} %fusion.35) | copy-start | bytes 1179652
